TPU v7x, 32 devices: a whole 2x2x4 slice. The times are simulated.
32 devices in a mesh: groups: 2 (over y), blk: 4 (over z), dp: 2 (over x), sub: 2 (over core).
Axes of the slice: x: 2, y: 2, z: 4, core: 2. Of those that a mesh axis runs over, the one named last changes fastest.
Arguments:
- view_a: bfloat16 [2048, 256], P(('groups', 'blk', 'dp', 'sub')), parts along dimension 0, may hold values from -6 to 6
- view_b: bfloat16 [2048, 256], P(('groups', 'blk', 'dp', 'sub')), parts along dimension 0, may hold values from -6 to 6
- prototypes: bfloat16 [32768, 256], P('blk'), may hold values from -6 to 6
- tile_mask: int32 [16, 256], replicated, may hold values from 0 to 1, as said below
- tile_region: int32 [32], P('groups'), parts along dimension 0, may hold values from 0 to 15, as said below
Outputs:
- grad_view_b: float32 [2048, 256], P(('groups', 'blk', 'dp', 'sub')), parts along dimension 0
- grad_prototypes: float32 [65536, 256], P(('groups', 'blk', 'dp', 'sub')), parts along dimension 0
There are 2 independent parts, one for each index of `groups`. A program takes and returns all parts, laid end to end along the dimension named above; an argument that names none is the same for every part. Nothing has to cross between parts.
Inputs may be any that keep to these rules, and one draw needn't show every extreme that they name: `tile_mask`: every prototype tile is 1 for at least one region, and every region for at least 16 tiles. `tile_region`: every region is named by at least one hit tile.
All inputs are finite; a program needn't handle non-finite values.
Results may differ from a plain program's by a relative error of at most 0.00045.
The roundings to bfloat16 on the way count: a program that leaves them out, or rounds other values in their place, can miss the bound.
Values may be sent and summed in bfloat16 or wider, within the bound.
A program may use at most 64 MiB of HBM per device.

v0:
```python
import jax
import jax.numpy as jnp
from jax import lax
from jax.sharding import PartitionSpec as P

TILE = 128
ITERS = 3
SOFTMAX_TEMPER = 0.1
EPSILON = 0.05


def from_behind(block, axis, distance):
    devices = range(lax.axis_size(axis))
    route = [((i - distance) % len(devices), i) for i in devices]
    return lax.ppermute(block, axis, route)


def unit_rows(matrix):
    values = matrix.astype(jnp.float32)
    return (values * lax.rsqrt(jnp.sum(values * values, axis=1, keepdims=True) + 1e-06)).astype(
        jnp.bfloat16
    )


def to_global(vector, blk_pos, block_count):
    return jnp.roll(vector[::-1], blk_pos + 1 - block_count, axis=0)


def body(view_a, view_b, prototypes, tile_mask, tile_region):
    n_blk = lax.axis_size("blk")
    n_dp = lax.axis_size("dp")
    n_sub = lax.axis_size("sub")
    blk_pos = lax.axis_index("blk")
    dp_pos = lax.axis_index("dp")
    sub_pos = lax.axis_index("sub")
    hit_dev = view_a.shape[0]
    block_rows = prototypes.shape[0]
    share_cols = block_rows // n_dp
    tiles_share = share_cols // TILE
    tiles_block = block_rows // TILE
    regions = tile_mask.shape[0]
    own_block = unit_rows(lax.dynamic_slice_in_dim(prototypes, dp_pos * share_cols, share_cols, 0))
    unit_a = unit_rows(view_a)
    unit_b = unit_rows(view_b)
    rows_a, rows_b = (
        lax.all_gather(unit_a, "dp", axis=0, tiled=True),
        lax.all_gather(unit_b, "dp", axis=0, tiled=True),
    )
    detector_hit_rows = rows_a.shape[0]
    both_rows = jnp.concatenate([rows_a, rows_b], axis=0)
    region_grid = tile_region.reshape(n_blk, n_dp, n_sub)
    my_regions = lax.dynamic_index_in_dim(
        lax.dynamic_index_in_dim(region_grid, blk_pos, 0, keepdims=False),
        sub_pos,
        1,
        keepdims=False,
    )
    onehot = (my_regions[:, None] == jnp.arange(regions, dtype=jnp.int32)[None, :]).astype(
        jnp.float32
    )
    row_tiles = jnp.dot(onehot, tile_mask.astype(jnp.float32))

    def active_at(block_id):
        tile_flags = lax.dynamic_slice_in_dim(
            row_tiles, block_id * tiles_block + dp_pos * tiles_share, tiles_share, 1
        )
        expanded = jnp.broadcast_to(
            tile_flags[:, None, :, None] > 0.5, (n_dp, hit_dev, tiles_share, TILE)
        )
        return expanded.reshape(detector_hit_rows, share_cols)

    def forward(proto_block, block_id):
        prototype_scores = jnp.einsum(
            "rd,kd->rk", both_rows, proto_block, preferred_element_type=jnp.float32
        )
        live_block_mask = active_at(block_id)
        code_exp = jnp.where(
            live_block_mask, jnp.exp((prototype_scores[:detector_hit_rows] - 1.0) / EPSILON), 0.0
        ).astype(jnp.bfloat16)
        prototype_weights = jnp.where(
            live_block_mask,
            jnp.exp((prototype_scores[detector_hit_rows:] - 1.0) / SOFTMAX_TEMPER),
            0.0,
        )
        return (
            code_exp,
            jnp.sum(code_exp.astype(jnp.float32), axis=0),
            jnp.sum(prototype_weights, axis=1),
        )

    code_first, colsum_first, norm_first = forward(own_block, blk_pos)
    code_stack = (
        jnp.zeros((n_blk, detector_hit_rows, share_cols), jnp.bfloat16).at[0].set(code_first)
    )
    colsum_stack = jnp.zeros((n_blk, share_cols), jnp.float32).at[0].set(colsum_first)
    block_stack = jnp.zeros((1,), jnp.bfloat16)

    def forward_turn(carry_state, turn_index):
        proto_block, code_all, colsum_all, blocks_all, norm_part = carry_state
        proto_block = from_behind(proto_block, "blk", 1)
        block_id = (blk_pos - turn_index) % n_blk
        code_exp, colsum, norm_add = forward(proto_block, block_id)
        code_all = lax.dynamic_update_index_in_dim(code_all, code_exp, turn_index, 0)
        colsum_all = lax.dynamic_update_index_in_dim(colsum_all, colsum, turn_index, 0)
        return ((proto_block, code_all, colsum_all, blocks_all, norm_part + norm_add), None)

    turns = jnp.arange(1, n_blk, dtype=jnp.int32)
    carry_state, unused = lax.scan(
        forward_turn, (own_block, code_stack, colsum_stack, block_stack, norm_first), turns
    )
    code_all = carry_state[1]
    colsum_all = carry_state[2]
    blocks_all = carry_state[3]
    norm_part = carry_state[4]

    def column_recip(colsum_steps):
        global_sums = to_global(colsum_steps, blk_pos, n_blk).reshape(-1)
        totals = lax.psum(global_sums, ("blk", "sub"))
        recip_vec = 1.0 / totals
        return to_global(recip_vec.reshape(n_blk, share_cols), blk_pos, n_blk)

    def row_partial(column_inverses):
        return jnp.sum(code_all.astype(jnp.float32) * column_inverses[:, None, :], axis=(0, 2))

    column_inverses = column_recip(colsum_all)
    row_totals, second_view_norm = lax.psum((row_partial(column_inverses), norm_part), "dp")
    row_inverses = 1.0 / row_totals
    for sweep_index in range(ITERS - 1):
        colsum_all = jnp.sum(code_all.astype(jnp.float32) * row_inverses[None, :, None], axis=1)
        column_inverses = column_recip(colsum_all)
        row_inverses = 1.0 / lax.psum(row_partial(column_inverses), "dp")

    def backward(proto_block, turn_index, block_id):
        prototype_scores = jnp.einsum(
            "rd,kd->rk", rows_b, proto_block, preferred_element_type=jnp.float32
        )
        live_block_mask = active_at(block_id)
        predicted_logits = (
            jnp.where(live_block_mask, jnp.exp((prototype_scores - 1.0) / SOFTMAX_TEMPER), 0.0)
            / second_view_norm[:, None]
        )
        code_exp = lax.dynamic_index_in_dim(code_all, turn_index, 0, keepdims=False).astype(
            jnp.float32
        )
        col_vals = lax.dynamic_index_in_dim(column_inverses, turn_index, 0, keepdims=False)
        code_entries = row_inverses[:, None] * code_exp * col_vals[None, :]
        score_gradient = ((predicted_logits - code_entries) / SOFTMAX_TEMPER).astype(jnp.bfloat16)
        hit_part = jnp.dot(score_gradient, proto_block, preferred_element_type=jnp.float32)
        proto_part = jnp.einsum(
            "rk,rd->kd", score_gradient, rows_b, preferred_element_type=jnp.float32
        )
        return (hit_part, proto_part)

    def pass_grads(running):
        return from_behind(running, "blk", 1)

    hit_first, proto_first = backward(own_block, 0, blk_pos)

    def backward_turn(carry_state, turn_index):
        proto_block, hit_running, proto_running = carry_state
        block_id = (blk_pos - turn_index) % n_blk
        proto_block = from_behind(proto_block, "blk", 1)
        proto_running = pass_grads(proto_running)
        hit_part, proto_part = backward(proto_block, turn_index, block_id)
        return ((proto_block, hit_running + hit_part, proto_running + proto_part), None)

    carry_state, unused = lax.scan(backward_turn, (own_block, hit_first, proto_first), turns)
    proto_home = pass_grads(carry_state[2])
    grad_view_b = lax.psum_scatter(carry_state[1], "dp", scatter_dimension=0, tiled=True)
    grad_prototypes = lax.psum_scatter(proto_home, "sub", scatter_dimension=0, tiled=True)
    return (grad_view_b, grad_prototypes)


def solution(mesh):
    placed = (
        P(("groups", "blk", "dp", "sub"), None),
        P(("groups", "blk", "dp", "sub"), None),
        P("blk", None),
        P(),
        P("groups"),
    )
    return jax.shard_map(
        body,
        mesh=mesh,
        in_specs=placed,
        out_specs=(
            P(("groups", "blk", "dp", "sub"), None),
            P(("groups", "blk", "dp", "sub"), None),
        ),
        check_vma=False,
    )
```

profile of v0, /device:TPU:0, one launch (start us, length us, event | category | flops | bytes accessed | tf_op | source)
XLA Modules:
  0.0 934.0 jit_solution(10555834925362059622)
XLA Ops:
  7.2 0.7 reshape.141
  8.0 2.2 fusion.28
  10.2 1.9 fusion.29
  12.4 5.5 all_gather.6
  18.1 4.6 all_gather.7
  22.7 1.4 copy.37
  24.1 2.7 fusion.61
  27.5 3.4 fusion.33
  30.9 2.4 scatter.6
  33.3 155.7 %while.37 = (s32[]{:T(128)}, bf16[4096,256]{1,0:T(8,128)(2,1)}, bf16[4,128,4096]{2,1,0:T(8,128)(2,1)}, f32[4,4096]{1,0:T(4,128)S(1)}, f32[128]{0:T(128)S(1)}, /*...) while((s32[]{:T(128)}, bf16[4096,256]{1,0:T(8,128)(2,1)}, ...), condition=%wide.region_8.9_spmd, body=%wide.region_5.8_spmd.sunk | while | flops 544206912 | bytes 27970340 | solution.py:108
  33.3 2.2 collective-permute-start
  38.9 42.1 %collective-permute-done = bf16[4096,256]{1,0:T(8,128)(2,1)S(1)} collective-permute-done((bf16[4096,256]{1,0:T(8,128)(2,1)}, bf16[4096,256]{1,0:T(8,128)(2,1)S(1)}, u32[]{:S(2)}, u32[]{:S(2)}) %collective-permute-start) | collective-permute-done | bytes 2097184 | tf_op jit(solution)/shard_map/while/body/eval_jaxpr/ppermute | solution.py:15
  81.1 0.7 fusion.93
  82.0 1.1 fusion.94
  83.2 1.6 bitcast_dynamic-update-slice_fusion.2
  85.0 1.4 copy.47
  89.8 43.0 %collective-permute-done = bf16[4096,256]{1,0:T(8,128)(2,1)S(1)} collective-permute-done((bf16[4096,256]{1,0:T(8,128)(2,1)}, bf16[4096,256]{1,0:T(8,128)(2,1)S(1)}, u32[]{:S(2)}, u32[]{:S(2)}) %collective-permute-start) | collective-permute-done | bytes 2097184 | tf_op jit(solution)/shard_map/while/body/eval_jaxpr/ppermute | solution.py:15
  133.8 1.1 fusion.94
  134.9 1.6 bitcast_dynamic-update-slice_fusion.2
  136.8 1.4 copy.47
  141.6 42.1 %collective-permute-done = bf16[4096,256]{1,0:T(8,128)(2,1)S(1)} collective-permute-done((bf16[4096,256]{1,0:T(8,128)(2,1)}, bf16[4096,256]{1,0:T(8,128)(2,1)S(1)}, u32[]{:S(2)}, u32[]{:S(2)}) %collective-permute-start) | collective-permute-done | bytes 2097184 | tf_op jit(solution)/shard_map/while/body/eval_jaxpr/ppermute | solution.py:15
  183.7 0.7 fusion.93
  184.6 1.1 fusion.94
  185.8 1.6 bitcast_dynamic-update-slice_fusion.2
  187.6 1.4 copy.47
  189.0 0.8 rev.18
  190.5 51.5 %all-reduce.7.cloned.1.call-done = f32[16384]{0:T(1024)} async-done(((f32[16384]{0:T(1024)}), f32[16384]{0:T(1024)}) %all-reduce.7.cloned.1.call-update) | async-done | bytes 65552 | tf_op jit(solution)/shard_map/psum | solution.py:118
  242.0 0.9 broadcast_divide_fusion.2
  242.9 0.8 rev.19
  243.8 3.1 fusion.16
  246.9 4.9 psum.51
  251.8 3.2 fusion.17
  255.0 0.8 rev.20
  256.6 52.7 %all-reduce.9.cloned.1.call-done = f32[16384]{0:T(1024)} async-done(((f32[16384]{0:T(1024)}), f32[16384]{0:T(1024)}) %all-reduce.9.cloned.1.call-update) | async-done | bytes 65552 | tf_op jit(solution)/shard_map/psum | solution.py:118
  309.3 0.9 broadcast_divide_fusion.1
  310.2 0.8 rev.21
  311.1 3.1 fusion.18
  314.2 4.9 psum.53
  319.1 3.2 fusion.19
  322.3 0.8 rev.22
  324.1 52.5 %all-reduce.11.cloned.1.call-done = f32[16384]{0:T(1024)} async-done(((f32[16384]{0:T(1024)}), f32[16384]{0:T(1024)}) %all-reduce.11.cloned.1.call-update) | async-done | bytes 65552 | tf_op jit(solution)/shard_map/psum | solution.py:118
  376.6 0.9 broadcast_divide_fusion
  377.5 0.8 rev.23
  378.4 3.2 fusion.20
  381.6 4.9 all-reduce.2
  386.6 2.5 fusion.27
  389.1 2.7 fusion.63
  392.3 435.9 %while.38 = (s32[]{:T(128)}, bf16[4096,256]{1,0:T(8,128)(2,1)S(1)}, f32[128,256]{1,0:T(8,128)S(1)}, f32[4096,256]{1,0:T(8,128)}, s32[3]{0:T(128)S(1)}, /*index=5...) while((s32[]{:T(128)}, bf16[4096,256]{1,0:T(8,128)(2,1)S(1)}, ...), condition=%wide.region_22.24_spmd, body=%wide.region_21.23_spmd.sunk | while | flops 811630720 | bytes 64407448 | solution.py:167
  397.7 131.2 %collective-permute-done.1 = bf16[4096,256]{1,0:T(8,128)(2,1)S(1)} collective-permute-done((bf16[4096,256]{1,0:T(8,128)(2,1)}, bf16[4096,256]{1,0:T(8,128)(2,1)S(1)}, u32[]{:S(2)}, u32[]{:S(2)}) %collective-permute-start.1) | collective-permute-done | bytes 2097184 | tf_op jit(solution)/shard_map/while/body/eval_jaxpr/ppermute | solution.py:15
  528.9 1.3 copy.63
  530.5 2.5 fusion.101
  533.5 5.1 convolution_add_fusion.7
  538.6 1.3 copy-done.2
  543.2 131.0 %collective-permute-done.1 = bf16[4096,256]{1,0:T(8,128)(2,1)S(1)} collective-permute-done((bf16[4096,256]{1,0:T(8,128)(2,1)}, bf16[4096,256]{1,0:T(8,128)(2,1)S(1)}, u32[]{:S(2)}, u32[]{:S(2)}) %collective-permute-start.1) | collective-permute-done | bytes 2097184 | tf_op jit(solution)/shard_map/while/body/eval_jaxpr/ppermute | solution.py:15
  674.2 1.3 copy.63
  675.7 2.5 fusion.101
  678.8 5.1 convolution_add_fusion.7
  683.9 1.3 copy-done.2
  688.5 130.1 %collective-permute-done.1 = bf16[4096,256]{1,0:T(8,128)(2,1)S(1)} collective-permute-done((bf16[4096,256]{1,0:T(8,128)(2,1)}, bf16[4096,256]{1,0:T(8,128)(2,1)S(1)}, u32[]{:S(2)}, u32[]{:S(2)}) %collective-permute-start.1) | collective-permute-done | bytes 2097184 | tf_op jit(solution)/shard_map/while/body/eval_jaxpr/ppermute | solution.py:15
  818.5 1.3 copy.63
  820.1 2.5 fusion.101
  823.1 5.1 convolution_add_fusion.7
  828.9 88.2 %collective-permute-done.3 = f32[4096,256]{1,0:T(8,128)} collective-permute-done((f32[4096,256]{1,0:T(8,128)}, f32[4096,256]{1,0:T(8,128)}, u32[]{:S(2)}, u32[]{:S(2)}) %collective-permute-start.3) | collective-permute-done | bytes 4194336 | tf_op jit(solution)/shard_map/ppermute | solution.py:15
  917.2 10.3 %reduce-scatter.5.cloned.1.call-done = f32[2048,256]{1,0:T(8,128)} async-done(((f32[4096,256]{1,0:T(8,128)}), f32[2048,256]{1,0:T(8,128)}) %reduce-scatter.5.cloned.1.call-update) | async-done | bytes 2097168 | tf_op jit(solution)/shard_map/reduce_scatter | solution.py:170
  (108 shorter events, 15.4 us)
Async XLA Ops:
  7.2 234.9 %all-reduce.7.cloned.1.call-start = ((), (), s32[]{:S(2)}) async-start(), calls=%async_computation.2 | async-start | bytes 131072 | tf_op jit(solution)/shard_map/psum | solution.py:118
  10.2 2.0 copy-start.5
  10.2 7.7 copy-start.6
  12.2 11.9 %copy-start = (bf16[4096,256]{1,0:T(8,128)(2,1)}, bf16[4096,256]{1,0:T(8,128)(2,1)S(1)}, u32[]{:S(2)}) copy-start(bf16[4096,256]{1,0:T(8,128)(2,1)S(1)} %fusion.29) | copy-start | bytes 6291460
  24.1 2.9 copy-start.7
  33.3 47.7 %collective-permute-start = (bf16[4096,256]{1,0:T(8,128)(2,1)}, bf16[4096,256]{1,0:T(8,128)(2,1)S(1)}, u32[]{:S(2)}, u32[]{:S(2)}) collective-permute-start(bf16[4096,256]{1,0:T(8,128)(2,1)} %get-tuple-element.575), channel_id=1, source_target_pairs={{12,0},{0,4},{4,8},{8,12},{13,1},{1,5},{5,9},{9,13},{14,2},{2,6},{... | collective-permute-start | bytes 6291464 | tf_op jit(solution)/shard_map/while/body/eval_jaxpr/ppermute | solution.py:15
  86.4 46.4 %collective-permute-start = (bf16[4096,256]{1,0:T(8,128)(2,1)}, bf16[4096,256]{1,0:T(8,128)(2,1)S(1)}, u32[]{:S(2)}, u32[]{:S(2)}) collective-permute-start(bf16[4096,256]{1,0:T(8,128)(2,1)} %get-tuple-element.575), channel_id=1, source_target_pairs={{12,0},{0,4},{4,8},{8,12},{13,1},{1,5},{5,9},{9,13},{14,2},{2,6},{... | collective-permute-start | bytes 6291464 | tf_op jit(solution)/shard_map/while/body/eval_jaxpr/ppermute | solution.py:15
  138.2 45.5 %collective-permute-start = (bf16[4096,256]{1,0:T(8,128)(2,1)}, bf16[4096,256]{1,0:T(8,128)(2,1)S(1)}, u32[]{:S(2)}, u32[]{:S(2)}) collective-permute-start(bf16[4096,256]{1,0:T(8,128)(2,1)} %get-tuple-element.575), channel_id=1, source_target_pairs={{12,0},{0,4},{4,8},{8,12},{13,1},{1,5},{5,9},{9,13},{14,2},{2,6},{... | collective-permute-start | bytes 6291464 | tf_op jit(solution)/shard_map/while/body/eval_jaxpr/ppermute | solution.py:15
  190.5 118.8 %all-reduce.9.cloned.1.call-start = ((), (), s32[]{:S(2)}) async-start(), calls=%async_computation.3 | async-start | bytes 131072 | tf_op jit(solution)/shard_map/psum | solution.py:118
  256.6 120.0 %all-reduce.11.cloned.1.call-start = ((), (), s32[]{:S(2)}) async-start(), calls=%async_computation.4 | async-start | bytes 131072 | tf_op jit(solution)/shard_map/psum | solution.py:118
  323.9 593.3 %reduce-scatter.3.cloned.1.call-start = ((), (), s32[]{:S(2)}) async-start(), calls=%async_computation.5 | async-start | bytes 196608 | tf_op jit(solution)/shard_map/reduce_scatter | solution.py:169
  378.4 8.2 copy-start.1
  392.3 1.3 copy-start.2
  392.4 141.1 %collective-permute-start.2 = (f32[4096,256]{1,0:T(8,128)}, f32[4096,256]{1,0:T(8,128)}, u32[]{:S(2)}, u32[]{:S(2)}) collective-permute-start(f32[4096,256]{1,0:T(8,128)} %get-tuple-element.628), channel_id=1, source_target_pairs={{12,0},{0,4},{4,8},{8,12},{13,1},{1,5},{5,9},{9,13},{14,2},{2,6},{... | collective-permute-start | bytes 12582920 | tf_op jit(solution)/shard_map/while/body/eval_jaxpr/ppermute | solution.py:15
  393.7 135.3 %collective-permute-start.1 = (bf16[4096,256]{1,0:T(8,128)(2,1)}, bf16[4096,256]{1,0:T(8,128)(2,1)S(1)}, u32[]{:S(2)}, u32[]{:S(2)}) collective-permute-start(bf16[4096,256]{1,0:T(8,128)(2,1)} %copy-done.2), channel_id=1, source_target_pairs={{12,0},{0,4},{4,8},{8,12},{13,1},{1,5},{5,9},{9,13},{14,2},{2,6},{... | collective-permute-start | bytes 6291464 | tf_op jit(solution)/shard_map/while/body/eval_jaxpr/ppermute | solution.py:15
  533.5 5.1 copy-start.3
  538.6 1.3 copy-start.2
  538.6 140.2 %collective-permute-start.2 = (f32[4096,256]{1,0:T(8,128)}, f32[4096,256]{1,0:T(8,128)}, u32[]{:S(2)}, u32[]{:S(2)}) collective-permute-start(f32[4096,256]{1,0:T(8,128)} %get-tuple-element.628), channel_id=1, source_target_pairs={{12,0},{0,4},{4,8},{8,12},{13,1},{1,5},{5,9},{9,13},{14,2},{2,6},{... | collective-permute-start | bytes 12582920 | tf_op jit(solution)/shard_map/while/body/eval_jaxpr/ppermute | solution.py:15
  539.9 134.3 %collective-permute-start.1 = (bf16[4096,256]{1,0:T(8,128)(2,1)}, bf16[4096,256]{1,0:T(8,128)(2,1)S(1)}, u32[]{:S(2)}, u32[]{:S(2)}) collective-permute-start(bf16[4096,256]{1,0:T(8,128)(2,1)} %copy-done.2), channel_id=1, source_target_pairs={{12,0},{0,4},{4,8},{8,12},{13,1},{1,5},{5,9},{9,13},{14,2},{2,6},{... | collective-permute-start | bytes 6291464 | tf_op jit(solution)/shard_map/while/body/eval_jaxpr/ppermute | solution.py:15
  678.8 5.1 copy-start.3
  683.9 1.3 copy-start.2
  683.9 139.2 %collective-permute-start.2 = (f32[4096,256]{1,0:T(8,128)}, f32[4096,256]{1,0:T(8,128)}, u32[]{:S(2)}, u32[]{:S(2)}) collective-permute-start(f32[4096,256]{1,0:T(8,128)} %get-tuple-element.628), channel_id=1, source_target_pairs={{12,0},{0,4},{4,8},{8,12},{13,1},{1,5},{5,9},{9,13},{14,2},{2,6},{... | collective-permute-start | bytes 12582920 | tf_op jit(solution)/shard_map/while/body/eval_jaxpr/ppermute | solution.py:15
  685.2 133.4 %collective-permute-start.1 = (bf16[4096,256]{1,0:T(8,128)(2,1)}, bf16[4096,256]{1,0:T(8,128)(2,1)S(1)}, u32[]{:S(2)}, u32[]{:S(2)}) collective-permute-start(bf16[4096,256]{1,0:T(8,128)(2,1)} %copy-done.2), channel_id=1, source_target_pairs={{12,0},{0,4},{4,8},{8,12},{13,1},{1,5},{5,9},{9,13},{14,2},{2,6},{... | collective-permute-start | bytes 6291464 | tf_op jit(solution)/shard_map/while/body/eval_jaxpr/ppermute | solution.py:15
  823.1 5.1 copy-start.3
  828.2 0.6 copy-start.4
  828.2 88.9 %collective-permute-start.3 = (f32[4096,256]{1,0:T(8,128)}, f32[4096,256]{1,0:T(8,128)}, u32[]{:S(2)}, u32[]{:S(2)}) collective-permute-start(f32[4096,256]{1,0:T(8,128)} %get-tuple-element.360), channel_id=1, source_target_pairs={{12,0},{0,4},{4,8},{8,12},{13,1},{1,5},{5,9},{9,13},{14,2},{2,6},{... | collective-permute-start | bytes 12582920 | tf_op jit(solution)/shard_map/ppermute | solution.py:15
  828.9 98.6 %reduce-scatter.5.cloned.1.call-start = ((), (), s32[]{:S(2)}) async-start(), calls=%async_computation.6 | async-start | bytes 6291456 | tf_op jit(solution)/shard_map/reduce_scatter | solution.py:170
Sparse Core Ops, SparseCore 0:
  190.6 51.3 all-reduce.6
  256.7 52.5 all-reduce.8
  324.0 52.5 all-reduce.10
  829.0 11.0 reduce-scatter.2
  917.3 10.2 reduce-scatter.4
where the time goes:
time: 935 us; the launch traced here: 934 us
  waiting for transfers between devices  775 us (83%)
  other arithmetic  35.5 us (4%)
  matrix products  35.1 us (4%)
  local copies, waits for them, and re-layouts  29.5 us (3%)
  blocking collectives  24.9 us (3%)
  loops' own time  16.2 us (2%)
  between operations  14.1 us (2%)
    ppermute x10, waiting for transfers between devices, from_behind(): return lax.ppermute(block, axis, route)  608 us
    psum x3, waiting for transfers between devices, column_recip(): totals = lax.psum(global_sums, ('blk', 'sub'))  157 us
  transfers between devices with their start and end apart: 15, of which 11 were waited for; matrix products, arithmetic and copies ran while one was open for 2% of the time, Pallas kernels for 0%

commit v1 on v0

--- a/solution.py
+++ b/solution.py
@@ -115,7 +115,7 @@
 
     def column_recip(colsum_steps):
         global_sums = to_global(colsum_steps, blk_pos, n_blk).reshape(-1)
-        totals = lax.psum(global_sums, ("blk", "sub"))
+        totals = jnp.sum(lax.all_gather(global_sums, ("blk", "sub")), axis=0)
         recip_vec = 1.0 / totals
         return to_global(recip_vec.reshape(n_blk, share_cols), blk_pos, n_blk)
 

time: 935 us -> 828 us (0.89)
  waiting for transfers between devices: 775 us -> 627 us
  blocking collectives: 24.9 us -> 70.1 us
    psum x3 -> x0, waiting for transfers between devices: 157 us -> none  [column_recip(): totals = lax.psum(global_sums, ('blk', 'sub'))]
    all_gather x0 -> x3, blocking collectives: none -> 45.2 us  [column_recip(): totals = jnp.sum(lax.all_gather(global_sums, ('blk', 'sub')), axis=0)]
  transfers between devices with their start and end apart: 15 -> 12, of which waited for: 11 -> 8; matrix products, arithmetic and copies ran while one was open for 2% -> 2% of each run, Pallas kernels for 0% -> 0%
where the time goes in v1:
time: 828 us
  waiting for transfers between devices  627 us (76%)
  blocking collectives  70.1 us (8%)
  matrix products  35.1 us (4%)
  other arithmetic  34.1 us (4%)
  local copies, waits for them, and re-layouts  28.6 us (3%)
  loops' own time  15.9 us (2%)
  between operations  14.4 us (2%)
    ppermute x10, waiting for transfers between devices, from_behind(): return lax.ppermute(block, axis, route)  617 us
    all_gather x3, blocking collectives, column_recip(): totals = jnp.sum(lax.all_gather(global_sums, ('blk', 'sub')), axis=0)  45.2 us
    dot_general x4, matrix products, backward(): jnp.einsum('rk,rd->kd', score_gradient, rows_b, preferred_element_type=jn...  18 us
  transfers between devices with their start and end apart: 12, of which 8 were waited for; matrix products, arithmetic and copies ran while one was open for 2% of the time, Pallas kernels for 0%

profile of v1, /device:TPU:0, one launch (start us, length us, event | category | flops | bytes accessed | tf_op | source)
XLA Modules:
  0.0 827.5 jit_solution(12113788238089828121)
XLA Ops:
  7.2 0.7 reshape.129
  8.0 2.2 fusion.28
  10.2 1.9 fusion.29
  12.4 5.5 all_gather.15
  18.1 4.6 all_gather.16
  22.7 1.4 copy.34
  24.1 2.7 fusion.58
  27.5 3.4 fusion.33
  30.9 2.4 scatter.6
  33.3 155.7 %while.37 = (s32[]{:T(128)}, bf16[4096,256]{1,0:T(8,128)(2,1)}, bf16[4,128,4096]{2,1,0:T(8,128)(2,1)}, f32[4,4096]{1,0:T(4,128)S(1)}, f32[128]{0:T(128)S(1)}, /*...) while((s32[]{:T(128)}, bf16[4096,256]{1,0:T(8,128)(2,1)}, ...), condition=%wide.region_8.9_spmd, body=%wide.region_5.8_spmd.sunk | while | flops 544206912 | bytes 27970340 | solution.py:108
  33.3 2.2 collective-permute-start
  38.9 42.1 %collective-permute-done = bf16[4096,256]{1,0:T(8,128)(2,1)S(1)} collective-permute-done((bf16[4096,256]{1,0:T(8,128)(2,1)}, bf16[4096,256]{1,0:T(8,128)(2,1)S(1)}, u32[]{:S(2)}, u32[]{:S(2)}) %collective-permute-start) | collective-permute-done | bytes 2097184 | tf_op jit(solution)/shard_map/while/body/eval_jaxpr/ppermute | solution.py:15
  81.1 0.7 fusion.90
  82.0 1.1 fusion.91
  83.1 1.6 bitcast_dynamic-update-slice_fusion.2
  85.0 1.4 copy.44
  89.8 43.0 %collective-permute-done = bf16[4096,256]{1,0:T(8,128)(2,1)S(1)} collective-permute-done((bf16[4096,256]{1,0:T(8,128)(2,1)}, bf16[4096,256]{1,0:T(8,128)(2,1)S(1)}, u32[]{:S(2)}, u32[]{:S(2)}) %collective-permute-start) | collective-permute-done | bytes 2097184 | tf_op jit(solution)/shard_map/while/body/eval_jaxpr/ppermute | solution.py:15
  132.8 0.7 fusion.90
  133.8 1.1 fusion.91
  134.9 1.6 bitcast_dynamic-update-slice_fusion.2
  136.8 1.4 copy.44
  141.6 42.1 %collective-permute-done = bf16[4096,256]{1,0:T(8,128)(2,1)S(1)} collective-permute-done((bf16[4096,256]{1,0:T(8,128)(2,1)}, bf16[4096,256]{1,0:T(8,128)(2,1)S(1)}, u32[]{:S(2)}, u32[]{:S(2)}) %collective-permute-start) | collective-permute-done | bytes 2097184 | tf_op jit(solution)/shard_map/while/body/eval_jaxpr/ppermute | solution.py:15
  183.7 0.7 fusion.90
  184.6 1.1 fusion.91
  185.8 1.6 bitcast_dynamic-update-slice_fusion.2
  187.6 1.4 copy.44
  189.0 0.8 rev.18
  189.9 15.0 %all-gather = f32[8,1,16384]{2,1,0:T(1,128)S(1)} all-gather(f32[1,1,16384]{2,1,0:T(1,128)S(1)} %reshape.135), channel_id=1, replica_groups=mesh['groups'=2,'blk'=4,'dp'=2,'sub'=2] {'blk','sub'}, dimensions={0}, use_global_device_ids=true | all-gather | bytes 589824 | tf_op jit(solution)/shard_map/all_gather | solution.py:118
  205.4 0.8 reverse.9
  206.3 3.1 fusion.16
  209.4 4.9 psum.29
  214.3 3.2 fusion.17
  217.5 0.8 rev.20
  218.5 15.2 %all-gather.1 = f32[8,1,16384]{2,1,0:T(1,128)S(1)} all-gather(f32[1,1,16384]{2,1,0:T(1,128)S(1)} %reshape.137), channel_id=1, replica_groups=mesh['groups'=2,'blk'=4,'dp'=2,'sub'=2] {'blk','sub'}, dimensions={0}, use_global_device_ids=true | all-gather | bytes 589824 | tf_op jit(solution)/shard_map/all_gather | solution.py:118
  234.1 0.8 reverse.10
  235.0 3.1 fusion.18
  238.1 4.9 psum.30
  243.0 3.2 fusion.19
  246.2 0.8 rev.22
  247.2 15.0 %all-gather.2 = f32[8,1,16384]{2,1,0:T(1,128)S(1)} all-gather(f32[1,1,16384]{2,1,0:T(1,128)S(1)} %reshape.139), channel_id=1, replica_groups=mesh['groups'=2,'blk'=4,'dp'=2,'sub'=2] {'blk','sub'}, dimensions={0}, use_global_device_ids=true | all-gather | bytes 589824 | tf_op jit(solution)/shard_map/all_gather | solution.py:118
  262.6 0.8 reverse.11
  263.5 3.2 fusion.20
  266.8 4.9 all-reduce.2
  271.7 2.5 fusion.27
  274.2 2.7 fusion.60
  277.4 442.2 %while.38 = (s32[]{:T(128)}, bf16[4096,256]{1,0:T(8,128)(2,1)S(1)}, f32[128,256]{1,0:T(8,128)S(1)}, f32[4096,256]{1,0:T(8,128)}, s32[3]{0:T(128)S(1)}, /*index=5...) while((s32[]{:T(128)}, bf16[4096,256]{1,0:T(8,128)(2,1)S(1)}, ...), condition=%wide.region_22.24_spmd, body=%wide.region_21.23_spmd.sunk | while | flops 811630720 | bytes 64407448 | solution.py:167
  277.5 1.2 copy-done.2
  278.8 0.6 dynamic_slice.154
  282.0 134.1 %collective-permute-done.1 = bf16[4096,256]{1,0:T(8,128)(2,1)S(1)} collective-permute-done((bf16[4096,256]{1,0:T(8,128)(2,1)}, bf16[4096,256]{1,0:T(8,128)(2,1)S(1)}, u32[]{:S(2)}, u32[]{:S(2)}) %collective-permute-start.1) | collective-permute-done | bytes 2097184 | tf_op jit(solution)/shard_map/while/body/eval_jaxpr/ppermute | solution.py:15
  416.1 1.3 copy.57
  417.7 2.5 fusion.98
  420.7 5.1 convolution_add_fusion.7
  425.8 1.3 copy-done.2
  430.4 133.1 %collective-permute-done.1 = bf16[4096,256]{1,0:T(8,128)(2,1)S(1)} collective-permute-done((bf16[4096,256]{1,0:T(8,128)(2,1)}, bf16[4096,256]{1,0:T(8,128)(2,1)S(1)}, u32[]{:S(2)}, u32[]{:S(2)}) %collective-permute-start.1) | collective-permute-done | bytes 2097184 | tf_op jit(solution)/shard_map/while/body/eval_jaxpr/ppermute | solution.py:15
  563.5 1.3 copy.57
  565.1 2.5 fusion.98
  568.1 5.1 convolution_add_fusion.7
  573.2 1.3 copy-done.2
  577.8 132.2 %collective-permute-done.1 = bf16[4096,256]{1,0:T(8,128)(2,1)S(1)} collective-permute-done((bf16[4096,256]{1,0:T(8,128)(2,1)}, bf16[4096,256]{1,0:T(8,128)(2,1)S(1)}, u32[]{:S(2)}, u32[]{:S(2)}) %collective-permute-start.1) | collective-permute-done | bytes 2097184 | tf_op jit(solution)/shard_map/while/body/eval_jaxpr/ppermute | solution.py:15
  710.0 1.3 copy.57
  711.5 2.5 fusion.98
  714.6 5.1 convolution_add_fusion.7
  720.4 90.3 %collective-permute-done.3 = f32[4096,256]{1,0:T(8,128)} collective-permute-done((f32[4096,256]{1,0:T(8,128)}, f32[4096,256]{1,0:T(8,128)}, u32[]{:S(2)}, u32[]{:S(2)}) %collective-permute-start.3) | collective-permute-done | bytes 4194336 | tf_op jit(solution)/shard_map/ppermute | solution.py:15
  810.7 10.0 %reduce-scatter.5.cloned.1.call-done = f32[2048,256]{1,0:T(8,128)} async-done(((f32[4096,256]{1,0:T(8,128)}), f32[2048,256]{1,0:T(8,128)}) %reduce-scatter.5.cloned.1.call-update) | async-done | bytes 2097168 | tf_op jit(solution)/shard_map/reduce_scatter | solution.py:170
  (105 shorter events, 11.5 us)
Async XLA Ops:
  7.2 803.5 %reduce-scatter.3.cloned.1.call-start = ((), (), s32[]{:S(2)}) async-start(), calls=%async_computation.2 | async-start | bytes 196608 | tf_op jit(solution)/shard_map/reduce_scatter | solution.py:169
  10.2 2.0 copy-start.5
  10.2 7.7 copy-start.6
  12.2 11.9 %copy-start = (bf16[4096,256]{1,0:T(8,128)(2,1)}, bf16[4096,256]{1,0:T(8,128)(2,1)S(1)}, u32[]{:S(2)}) copy-start(bf16[4096,256]{1,0:T(8,128)(2,1)S(1)} %fusion.29) | copy-start | bytes 6291460
  24.1 2.9 copy-start.7
  33.3 47.7 %collective-permute-start = (bf16[4096,256]{1,0:T(8,128)(2,1)}, bf16[4096,256]{1,0:T(8,128)(2,1)S(1)}, u32[]{:S(2)}, u32[]{:S(2)}) collective-permute-start(bf16[4096,256]{1,0:T(8,128)(2,1)} %get-tuple-element.575), channel_id=1, source_target_pairs={{12,0},{0,4},{4,8},{8,12},{13,1},{1,5},{5,9},{9,13},{14,2},{2,6},{... | collective-permute-start | bytes 6291464 | tf_op jit(solution)/shard_map/while/body/eval_jaxpr/ppermute | solution.py:15
  86.4 46.4 %collective-permute-start = (bf16[4096,256]{1,0:T(8,128)(2,1)}, bf16[4096,256]{1,0:T(8,128)(2,1)S(1)}, u32[]{:S(2)}, u32[]{:S(2)}) collective-permute-start(bf16[4096,256]{1,0:T(8,128)(2,1)} %get-tuple-element.575), channel_id=1, source_target_pairs={{12,0},{0,4},{4,8},{8,12},{13,1},{1,5},{5,9},{9,13},{14,2},{2,6},{... | collective-permute-start | bytes 6291464 | tf_op jit(solution)/shard_map/while/body/eval_jaxpr/ppermute | solution.py:15
  138.2 45.5 %collective-permute-start = (bf16[4096,256]{1,0:T(8,128)(2,1)}, bf16[4096,256]{1,0:T(8,128)(2,1)S(1)}, u32[]{:S(2)}, u32[]{:S(2)}) collective-permute-start(bf16[4096,256]{1,0:T(8,128)(2,1)} %get-tuple-element.575), channel_id=1, source_target_pairs={{12,0},{0,4},{4,8},{8,12},{13,1},{1,5},{5,9},{9,13},{14,2},{2,6},{... | collective-permute-start | bytes 6291464 | tf_op jit(solution)/shard_map/while/body/eval_jaxpr/ppermute | solution.py:15
  263.5 8.2 copy-start.1
  277.5 1.3 copy-start.2
  277.5 143.2 %collective-permute-start.2 = (f32[4096,256]{1,0:T(8,128)}, f32[4096,256]{1,0:T(8,128)}, u32[]{:S(2)}, u32[]{:S(2)}) collective-permute-start(f32[4096,256]{1,0:T(8,128)} %get-tuple-element.628), channel_id=1, source_target_pairs={{12,0},{0,4},{4,8},{8,12},{13,1},{1,5},{5,9},{9,13},{14,2},{2,6},{... | collective-permute-start | bytes 12582920 | tf_op jit(solution)/shard_map/while/body/eval_jaxpr/ppermute | solution.py:15
  278.8 137.4 %collective-permute-start.1 = (bf16[4096,256]{1,0:T(8,128)(2,1)}, bf16[4096,256]{1,0:T(8,128)(2,1)S(1)}, u32[]{:S(2)}, u32[]{:S(2)}) collective-permute-start(bf16[4096,256]{1,0:T(8,128)(2,1)} %copy-done.2), channel_id=1, source_target_pairs={{12,0},{0,4},{4,8},{8,12},{13,1},{1,5},{5,9},{9,13},{14,2},{2,6},{... | collective-permute-start | bytes 6291464 | tf_op jit(solution)/shard_map/while/body/eval_jaxpr/ppermute | solution.py:15
  420.7 5.1 copy-start.3
  425.8 1.3 copy-start.2
  425.8 142.3 %collective-permute-start.2 = (f32[4096,256]{1,0:T(8,128)}, f32[4096,256]{1,0:T(8,128)}, u32[]{:S(2)}, u32[]{:S(2)}) collective-permute-start(f32[4096,256]{1,0:T(8,128)} %get-tuple-element.628), channel_id=1, source_target_pairs={{12,0},{0,4},{4,8},{8,12},{13,1},{1,5},{5,9},{9,13},{14,2},{2,6},{... | collective-permute-start | bytes 12582920 | tf_op jit(solution)/shard_map/while/body/eval_jaxpr/ppermute | solution.py:15
  427.1 136.4 %collective-permute-start.1 = (bf16[4096,256]{1,0:T(8,128)(2,1)}, bf16[4096,256]{1,0:T(8,128)(2,1)S(1)}, u32[]{:S(2)}, u32[]{:S(2)}) collective-permute-start(bf16[4096,256]{1,0:T(8,128)(2,1)} %copy-done.2), channel_id=1, source_target_pairs={{12,0},{0,4},{4,8},{8,12},{13,1},{1,5},{5,9},{9,13},{14,2},{2,6},{... | collective-permute-start | bytes 6291464 | tf_op jit(solution)/shard_map/while/body/eval_jaxpr/ppermute | solution.py:15
  568.1 5.1 copy-start.3
  573.2 1.3 copy-start.2
  573.2 141.4 %collective-permute-start.2 = (f32[4096,256]{1,0:T(8,128)}, f32[4096,256]{1,0:T(8,128)}, u32[]{:S(2)}, u32[]{:S(2)}) collective-permute-start(f32[4096,256]{1,0:T(8,128)} %get-tuple-element.628), channel_id=1, source_target_pairs={{12,0},{0,4},{4,8},{8,12},{13,1},{1,5},{5,9},{9,13},{14,2},{2,6},{... | collective-permute-start | bytes 12582920 | tf_op jit(solution)/shard_map/while/body/eval_jaxpr/ppermute | solution.py:15
  574.5 135.5 %collective-permute-start.1 = (bf16[4096,256]{1,0:T(8,128)(2,1)}, bf16[4096,256]{1,0:T(8,128)(2,1)S(1)}, u32[]{:S(2)}, u32[]{:S(2)}) collective-permute-start(bf16[4096,256]{1,0:T(8,128)(2,1)} %copy-done.2), channel_id=1, source_target_pairs={{12,0},{0,4},{4,8},{8,12},{13,1},{1,5},{5,9},{9,13},{14,2},{2,6},{... | collective-permute-start | bytes 6291464 | tf_op jit(solution)/shard_map/while/body/eval_jaxpr/ppermute | solution.py:15
  714.5 5.1 copy-start.3
  719.6 0.6 copy-start.4
  719.6 91.0 %collective-permute-start.3 = (f32[4096,256]{1,0:T(8,128)}, f32[4096,256]{1,0:T(8,128)}, u32[]{:S(2)}, u32[]{:S(2)}) collective-permute-start(f32[4096,256]{1,0:T(8,128)} %get-tuple-element.360), channel_id=1, source_target_pairs={{12,0},{0,4},{4,8},{8,12},{13,1},{1,5},{5,9},{9,13},{14,2},{2,6},{... | collective-permute-start | bytes 12582920 | tf_op jit(solution)/shard_map/ppermute | solution.py:15
  720.3 100.4 %reduce-scatter.5.cloned.1.call-start = ((), (), s32[]{:S(2)}) async-start(), calls=%async_computation.3 | async-start | bytes 6291456 | tf_op jit(solution)/shard_map/reduce_scatter | solution.py:170
Sparse Core Ops, SparseCore 0:
  720.4 10.6 reduce-scatter.2
  810.8 9.8 reduce-scatter.4
